TPU v7x, 256 devices: a whole 4x4x8 slice. The times are simulated.
256 devices in a mesh: prow: 32 (over x, z), pcol: 8 (over y, core).
Axes of the slice: x: 4, y: 4, z: 8, core: 2. Of those that a mesh axis runs over, the one named last changes fastest.
Arguments:
- anc_inverse: bfloat16 [4, 32, 256, 16, 8, 256], P(None, 'prow', None, None, 'pcol'), may hold values from -6 to 6
- first_lower: bfloat16 [4, 32, 256, 256], P(None, 'prow', 'pcol'), may hold values from -0.046875 to 0.046875
- second_lower: bfloat16 [4, 32, 256, 256], P(None, 'prow', 'pcol'), may hold values from -0.0546875 to 0.0546875
- second_top: bfloat16 [256, 256], replicated, may hold values from -0.3125 to 0.3125
- struct_first: int32 [128], replicated, may hold values from 0 to 1
- struct_keep: int32 [128], replicated, may hold values from 0 to 1
- pivot_h: float32 [2, 256, 256], replicated, as said below
- pivot_s: float32 [2, 256, 256], replicated, as said below
- shifts: float32 [40], replicated, may hold values from 0.5 to 4
- pole_index: int32 [40], replicated, may hold values from 0 to 39, each once
Outputs:
- first_column: bfloat16 [4, 32, 256, 256], P(None, 'prow', 'pcol')
- first_diag: float32 [256, 256], replicated
- link_column: bfloat16 [256, 256], replicated
- second_column: bfloat16 [4, 32, 256, 256], P(None, 'prow', 'pcol')
- second_diag: float32 [256, 256], replicated
Inputs may be any that keep to these rules, and one draw needn't show every extreme that they name: `struct_first`: 1 marks a block row of the first supernode's structure. `struct_keep`: 1 marks a structure block that the second supernode keeps. `pole_index`: each pole appears once. `pivot_h`: symmetric, with a positive diagonal larger than each row's off-diagonal magnitudes together. `pivot_s`: symmetric, with a positive diagonal larger than each row's off-diagonal magnitudes together.
All inputs are finite; a program needn't handle non-finite values.
Results may differ from a plain program's by a relative error of at most 0.0041.
The roundings to bfloat16 on the way count: a program that leaves them out, or rounds other values in their place, can miss the bound.
Values may be sent and summed in bfloat16 or wider, within the bound.
A program may use at most 64 MiB of HBM per device.

v0:
```python
import jax
import jax.numpy as jnp
from jax import lax
from jax.sharding import PartitionSpec as P


def pivot_inverse(h_block, s_block, shift):
    factor = jnp.linalg.cholesky(h_block + shift * s_block)
    identity = jnp.eye(h_block.shape[0], dtype=jnp.float32)
    return jax.scipy.linalg.cho_solve((factor, True), identity)


def local_mask(flags, row_blocks, grid_rows, my_row):
    table = flags.reshape(row_blocks, grid_rows).astype(jnp.float32)
    return lax.dynamic_index_in_dim(table, my_row, axis=1, keepdims=False)


def per_device(
    anc_inverse,
    first_lower,
    second_lower,
    second_top,
    struct_first,
    struct_keep,
    pivot_h,
    pivot_s,
    shifts,
    pole_index,
):
    grid_rows = lax.axis_size("prow")
    grid_cols = lax.axis_size("pcol")
    my_row = lax.axis_index("prow")
    my_col = lax.axis_index("pcol")
    row_blocks = first_lower.shape[0]
    slab = first_lower.shape[2]
    width = first_lower.shape[3]
    col_blocks = anc_inverse.shape[3]
    first_mask = local_mask(struct_first, row_blocks, grid_rows, my_row)
    second_mask = first_mask * local_mask(struct_keep, row_blocks, grid_rows, my_row)
    lower_first = first_lower[:, 0] * first_mask.astype(jnp.bfloat16)[:, None, None]
    lower_second = second_lower[:, 0] * second_mask.astype(jnp.bfloat16)[:, None, None]
    stacked = jnp.concatenate([lower_first, lower_second], axis=2)[:, None]
    gathered = lax.all_gather(stacked, "prow", axis=1, tiled=True)
    grouped = gathered.reshape(row_blocks, grid_rows // grid_cols, grid_cols, slab, 2 * width)
    columns = lax.all_to_all(grouped, "pcol", split_axis=2, concat_axis=3, tiled=True)
    column_blocks = columns.reshape(col_blocks, width, 2 * width)
    inverse_rows = anc_inverse.reshape(row_blocks, width, col_blocks, width)
    totals = lax.psum(
        jnp.einsum(
            "axcy,cyz->xaz", inverse_rows, column_blocks, preferred_element_type=jnp.float32
        ),
        "pcol",
    )
    row_part = lax.dynamic_slice_in_dim(totals, my_col * slab, slab, 0)
    first_col = (-row_part[:, :, :width] * first_mask[None, :, None]).astype(jnp.bfloat16)
    bridge = jnp.einsum("raw,wz->raz", first_col, second_top, preferred_element_type=jnp.float32)
    second_col = (-(row_part[:, :, width:] + bridge) * second_mask[None, :, None]).astype(
        jnp.bfloat16
    )
    first_rows = lower_first.transpose(1, 0, 2)
    second_rows = lower_second.transpose(1, 0, 2)
    first_term = jnp.einsum(
        "ray,raz->yz", first_rows, first_col, preferred_element_type=jnp.float32
    )
    cross_term = jnp.einsum(
        "ray,raz->yz", first_col, second_rows, preferred_element_type=jnp.float32
    )
    second_term = jnp.einsum(
        "ray,raz->yz", second_rows, second_col, preferred_element_type=jnp.float32
    )
    first_sum, cross_sum, second_sum = lax.psum(
        (first_term, cross_term, second_term), ("prow", "pcol")
    )
    poles = jnp.arange(shifts.shape[0], dtype=jnp.int32)
    shift = jnp.sum(jnp.where(poles == pole_index[0], shifts, 0.0))
    first_diag = pivot_inverse(pivot_h[0], pivot_s[0], shift) - first_sum
    link_col = (
        -(
            cross_sum
            + jnp.dot(
                first_diag.astype(jnp.bfloat16), second_top, preferred_element_type=jnp.float32
            )
        )
    ).astype(jnp.bfloat16)
    second_diag = (
        pivot_inverse(pivot_h[1], pivot_s[1], shift)
        - second_sum
        - jnp.einsum("yz,yw->zw", second_top, link_col, preferred_element_type=jnp.float32)
    )
    return (
        first_col.transpose(1, 0, 2)[:, None],
        first_diag,
        link_col,
        second_col.transpose(1, 0, 2)[:, None],
        second_diag,
    )


def solution(mesh):
    return jax.shard_map(
        per_device,
        mesh=mesh,
        in_specs=(
            P(None, "prow", None, None, "pcol", None),
            P(None, "prow", "pcol", None),
            P(None, "prow", "pcol", None),
            P(),
            P(),
            P(),
            P(),
            P(),
            P(),
            P(),
        ),
        out_specs=(P(None, "prow", "pcol", None), P(), P(), P(None, "prow", "pcol", None), P()),
        check_vma=False,
    )
```

profile of v0, /device:TPU:8, one launch (start us, length us, event | category | flops | bytes accessed | tf_op | source)
XLA Modules:
  0.0 544.1 jit_solution(14048645056738182097)
XLA Ops:
  7.2 0.7 convert_element_type.47
  8.0 0.7 convert_element_type.44
  8.7 0.2 dynamic-slice_reduce_fusion
  9.0 0.9 bitcast_multiply_fusion
  9.9 0.9 bitcast_multiply_fusion.1
  10.8 0.7 pad_maximum_fusion
  11.5 1.1 fusion.48
  12.7 1.1 fusion.47
  13.9 1.9 fusion.43
  15.8 0.7 fusion.23
  16.9 0.7 fusion.22
  17.7 0.7 fusion.11
  18.5 11.7 %cholesky.130 = f32[128,128]{1,0:T(8,128)S(1)} custom-call(f32[128,128]{1,0:T(8,128)S(1)} %cholesky.194), custom_call_target="Cholesky" | custom-call | tf_op jit(solution)/shard_map/jit(cholesky)/cholesky | solution.py:8
  30.3 9.8 %custom-call.15 = f32[1,128,128]{1,2,0:T(8,128)S(1)} custom-call(f32[1,128,128]{2,1,0:T(8,128)S(1)} %get-tuple-element.84), custom_call_target="InvertDiagBlocksLowerTriangular" | custom-call | tf_op jit(solution)/shard_map/jit(cholesky)/cholesky | solution.py:8
  40.3 0.3 convolution_subtract_fusion.5
  40.6 11.7 %cholesky.147 = f32[128,128]{1,0:T(8,128)S(1)} custom-call(f32[128,128]{1,0:T(8,128)S(1)} %convolution_subtract_fusion.5), custom_call_target="Cholesky" | custom-call | tf_op jit(solution)/shard_map/jit(cholesky)/cholesky | solution.py:8
  52.3 0.6 compare_reduce_fusion.3
  53.0 0.6 compare_reduce_fusion.2
  55.0 41.5 %all-gather.3.cloned.1.call-done = bf16[4,1024,512]{2,1,0:T(8,128)(2,1)} async-done(((bf16[4,32,512]{2,1,0:T(8,128)(2,1)}), bf16[4,1024,512]{2,1,0:T(8,128)(2,1)}) %all-gather.3.cloned.1.call-update) | async-done | bytes 4194320 | tf_op jit(solution)/shard_map/all_gather | solution.py:43
  96.5 4.7 copy.82
  101.2 5.2 all-to-all-start
  106.4 4.0 while.4
  106.5 0.6 fusion.74
  107.0 1.4 bitcast_dynamic-update-slice_fusion.4
  108.5 0.6 fusion.74
  109.0 1.4 bitcast_dynamic-update-slice_fusion.4
  110.4 19.7 %custom-call.16 = f32[2,128,128]{1,2,0:T(8,128)S(1)} custom-call(f32[2,128,128]{2,1,0:T(8,128)S(1)} %get-tuple-element.21), custom_call_target="InvertDiagBlocksLowerTriangular" | custom-call | tf_op jit(solution)/shard_map/jit(_cho_solve)/triangular_solve | solution.py:10
  130.1 11.7 %cholesky.164 = f32[128,128]{1,0:T(8,128)S(1)} custom-call(f32[128,128]{1,0:T(8,128)S(1)} %cholesky.197), custom_call_target="Cholesky" | custom-call | tf_op jit(solution)/shard_map/jit(cholesky)/cholesky | solution.py:8
  141.9 9.8 %custom-call.17 = f32[1,128,128]{1,2,0:T(8,128)S(1)} custom-call(f32[1,128,128]{2,1,0:T(8,128)S(1)} %get-tuple-element.80), custom_call_target="InvertDiagBlocksLowerTriangular" | custom-call | tf_op jit(solution)/shard_map/jit(cholesky)/cholesky | solution.py:8
  151.9 0.3 convolution_subtract_fusion.4
  152.2 11.7 %cholesky.181 = f32[128,128]{1,0:T(8,128)S(1)} custom-call(f32[128,128]{1,0:T(8,128)S(1)} %convolution_subtract_fusion.4), custom_call_target="Cholesky" | custom-call | tf_op jit(solution)/shard_map/jit(cholesky)/cholesky | solution.py:8
  163.9 0.6 compare_reduce_fusion.1
  164.6 0.6 compare_reduce_fusion
  166.6 4.0 while.5
  166.6 0.6 fusion.75
  167.2 1.4 bitcast_dynamic-update-slice_fusion.5
  168.6 0.6 fusion.75
  169.2 1.4 bitcast_dynamic-update-slice_fusion.5
  170.6 19.9 %custom-call.18 = f32[2,128,128]{1,2,0:T(8,128)S(1)} custom-call(f32[2,128,128]{2,1,0:T(8,128)S(1)} %get-tuple-element.22), custom_call_target="InvertDiagBlocksLowerTriangular" | custom-call | tf_op jit(solution)/shard_map/jit(_cho_solve)/triangular_solve | solution.py:10
  190.5 0.3 fusion.20
  190.9 0.3 convolution_subtract_fusion.3
  191.1 0.3 fusion.35
  191.4 0.3 fusion.34
  191.7 0.3 convolution_subtract_fusion.2
  192.0 0.3 fusion.33
  192.3 2.5 copy.83
  194.8 9.6 %fusion.2 = f32[256,4,512]{2,0,1:T(8,128)} fusion(bf16[16,256,512,1]{2,1,0,3:T(8,128)(2,1)S(1)} %bitcast.134, bf16[4,256,16,256]{3,2,1,0:T(8,128)(2,1)} %bitcast.136), kind=kOutput, calls=%fused_computation.6 | convolution fusion | flops 4294967296 | bytes 14680064 | tf_op jit(solution)/shard_map/axcy,cyz->xaz/dot_general | solution.py:49
  204.5 0.3 fusion.18
  204.8 0.3 convolution_subtract_fusion.1
  205.1 0.3 fusion.38
  205.4 0.3 fusion.37
  205.6 0.3 convolution_subtract_fusion
  206.0 64.4 %all-reduce.5.cloned.1.call-done = f32[256,4,512]{2,0,1:T(8,128)} async-done(((f32[256,4,512]{2,0,1:T(8,128)}), f32[256,4,512]{2,0,1:T(8,128)}) %all-reduce.5.cloned.1.call-update) | async-done | bytes 2097168 | tf_op jit(solution)/shard_map/psum | solution.py:48
  270.3 1.0 fusion.15
  271.3 0.9 convolution_bitcast_fusion.3
  272.2 0.9 convolution_bitcast_fusion.2
  273.1 1.1 fusion.10
  274.2 0.9 convolution_bitcast_fusion.1
  275.2 0.3 fusion.36
  275.5 1.6 fusion.71
  277.1 256.3 %all-reduce.7.cloned.1.call-done = (f32[256,256]{1,0:T(8,128)}, f32[256,256]{1,0:T(8,128)}, f32[256,256]{1,0:T(8,128)}) async-done(((f32[256,256]{1,0:T(8,128)}, f32[256,256]{1,0:T(8,128)}, f32[256,256]{1,0:T(8,128)}), (f32[256,256]{1,0:T(8,128)}, f32[256,256]{1,0:T(8,128)}, f32[256,256]{1,0:T(8,128)})) %all-reduce.7.cloned.1.call-update) | async-done | bytes 786448 | tf_op jit(solution)/shard_map/psum | solution.py:71
  533.4 1.0 maximum_subtract_fusion
  534.4 1.2 fusion.7
  535.6 1.9 fusion.6
  (45 shorter events, 1.9 us)
Async XLA Ops:
  7.2 266.0 %copy-start = (bf16[256,256]{1,0:T(8,128)(2,1)S(1)}, bf16[256,256]{1,0:T(8,128)(2,1)}, u32[]{:S(2)}) copy-start(bf16[256,256]{1,0:T(8,128)(2,1)} %param.16) | copy-start | bytes 393220
  7.2 89.3 %all-gather.3.cloned.1.call-start = ((), (), s32[]{:S(2)}) async-start(), calls=%async_computation.2 | async-start | bytes 4325376 | tf_op jit(solution)/shard_map/all_gather | solution.py:43
  101.2 91.1 %all-to-all-start = ((bf16[4,4,8,32,512]{4,3,1,0,2:T(8,128)(2,1)}), bf16[4,4,8,32,512]{4,3,1,0,2:T(8,128)(2,1)}, u32[]{:S(2)}, u32[]{:S(2)}) async-start(bf16[4,4,8,32,512]{4,3,1,0,2:T(8,128)(2,1)} %copy.82), calls=%async_computation | async-start | bytes 8388608 | tf_op jit(solution)/shard_map/all_to_all | solution.py:45
  106.4 164.0 %all-reduce.5.cloned.1.call-start = ((), (), s32[]{:S(2)}) async-start(), calls=%async_computation.1 | async-start | bytes 4194304 | tf_op jit(solution)/shard_map/psum | solution.py:48
  204.4 329.0 %all-reduce.7.cloned.1.call-start = ((), (), s32[]{:S(2)}) async-start(), calls=%async_computation.3 | async-start | bytes 1572864 | tf_op jit(solution)/shard_map/psum | solution.py:71
  274.2 263.3 %copy-start.3 = (bf16[32,4,256]{2,0,1:T(8,128)(2,1)}, bf16[32,4,256]{2,0,1:T(8,128)(2,1)S(1)}, u32[]{:S(2)}) copy-start(bf16[32,4,256]{2,0,1:T(8,128)(2,1)S(1)} %fusion.10) | copy-start | bytes 196612
  534.4 3.2 copy-start.1
  535.6 2.0 copy-start.2
Sparse Core Ops, SparseCore 0:
  11.6 84.8 all-gather.2
  204.5 65.7 all-reduce.4
  276.7 256.6 all-reduce.6
where the time goes:
time: 545 us; the launch traced here: 544 us
  waiting for transfers between devices  362 us (66%)
  other arithmetic  120 us (22%)
  matrix products  20.9 us (4%)
  local copies, waits for them, and re-layouts  18.6 us (3%)
  between operations  16.7 us (3%)
    psum x1, waiting for transfers between devices, per_device(): lax.psum((first_term, cross_term, second_term), ('prow', 'pcol'))  256 us
    another operation x14, other arithmetic, pivot_inverse(): factor = jnp.linalg.cholesky(h_block + shift * s_block)  69.2 us
    psum x1, waiting for transfers between devices, per_device(): lax.psum(jnp.einsum('axcy,cyz->xaz', inverse_rows, column_blocks, preferr...  64.4 us
    all_gather x1, waiting for transfers between devices, per_device(): gathered = lax.all_gather(stacked, 'prow', axis=1, tiled=True)  41.5 us
    another operation x5, other arithmetic, pivot_inverse(): return jax.scipy.linalg.cho_solve((factor, True), identity)  39.6 us
  transfers between devices with their start and end apart: 4, of which 3 were waited for; matrix products, arithmetic and copies ran while one was open for 24% of the time, Pallas kernels for 0%

commit v1 on v0

--- a/solution.py
+++ b/solution.py
@@ -69,7 +69,7 @@
         "ray,raz->yz", second_rows, second_col, preferred_element_type=jnp.float32
     )
     first_sum, cross_sum, second_sum = lax.psum(
-        (first_term, cross_term, second_term), ("prow", "pcol")
+        lax.psum((first_term, cross_term, second_term), "prow"), "pcol"
     )
     poles = jnp.arange(shifts.shape[0], dtype=jnp.int32)
     shift = jnp.sum(jnp.where(poles == pole_index[0], shifts, 0.0))

time: 545 us -> 485 us (0.89)
  waiting for transfers between devices: 362 us -> 301 us
    psum x1 -> x2, waiting for transfers between devices: 256 us -> 212 us  [the longest x1 150 us: per_device(): lax.psum((first_term, cross_term, second_term), 'prow')]
    psum x1, waiting for transfers between devices: 64.4 us -> 44.7 us  [per_device(): lax.psum(jnp.einsum('axcy,cyz->xaz', inverse_rows, column_blocks, preferr...]
  transfers between devices with their start and end apart: 4 -> 5, of which waited for: 3 -> 4; matrix products, arithmetic and copies ran while one was open for 24% -> 27% of each run, Pallas kernels for 0% -> 0%
where the time goes in v1:
time: 485 us; the launch traced here: 482 us
  waiting for transfers between devices  301 us (62%)
  other arithmetic  120 us (25%)
  matrix products  21.2 us (4%)
  local copies, waits for them, and re-layouts  18.6 us (4%)
  between operations  16.8 us (3%)
  starting transfers between devices  5.09 us (1%)
    psum x1, waiting for transfers between devices, per_device(): lax.psum((first_term, cross_term, second_term), 'prow')  150 us
    another operation x14, other arithmetic, pivot_inverse(): factor = jnp.linalg.cholesky(h_block + shift * s_block)  69.2 us
    psum x1, waiting for transfers between devices, per_device(): lax.psum(lax.psum((first_term, cross_term, second_term), 'prow'), 'pcol')  62.4 us
    psum x1, waiting for transfers between devices, per_device(): lax.psum(jnp.einsum('axcy,cyz->xaz', inverse_rows, column_blocks, preferr...  44.7 us
    all_gather x1, waiting for transfers between devices, per_device(): gathered = lax.all_gather(stacked, 'prow', axis=1, tiled=True)  43.5 us
    another operation x5, other arithmetic, pivot_inverse(): return jax.scipy.linalg.cho_solve((factor, True), identity)  39.4 us
    dot_general x1, matrix products, per_device(): jnp.einsum('axcy,cyz->xaz', inverse_rows, column_blocks, preferred_elemen...  9.8 us
  transfers between devices with their start and end apart: 5, of which 4 were waited for; matrix products, arithmetic and copies ran while one was open for 27% of the time, Pallas kernels for 0%

profile of v1, /device:TPU:8, one launch (start us, length us, event | category | flops | bytes accessed | tf_op | source)
XLA Modules:
  0.0 482.4 jit_solution(2449880050066863502)
XLA Ops:
  7.2 0.7 convert_element_type.47
  8.0 0.7 convert_element_type.44
  9.0 0.9 bitcast_multiply_fusion
  9.9 0.9 bitcast_multiply_fusion.1
  10.8 0.7 pad_maximum_fusion
  11.5 1.1 fusion.48
  12.7 1.1 fusion.47
  13.9 1.9 fusion.43
  15.8 0.7 fusion.23
  16.9 0.7 fusion.22
  17.7 0.7 fusion.11
  18.5 11.7 %cholesky.130 = f32[128,128]{1,0:T(8,128)S(1)} custom-call(f32[128,128]{1,0:T(8,128)S(1)} %cholesky.194), custom_call_target="Cholesky" | custom-call | tf_op jit(solution)/shard_map/jit(cholesky)/cholesky | solution.py:8
  30.3 9.8 %custom-call.15 = f32[1,128,128]{1,2,0:T(8,128)S(1)} custom-call(f32[1,128,128]{2,1,0:T(8,128)S(1)} %get-tuple-element.87), custom_call_target="InvertDiagBlocksLowerTriangular" | custom-call | tf_op jit(solution)/shard_map/jit(cholesky)/cholesky | solution.py:8
  40.3 0.3 convolution_subtract_fusion.5
  40.6 11.7 %cholesky.147 = f32[128,128]{1,0:T(8,128)S(1)} custom-call(f32[128,128]{1,0:T(8,128)S(1)} %convolution_subtract_fusion.5), custom_call_target="Cholesky" | custom-call | tf_op jit(solution)/shard_map/jit(cholesky)/cholesky | solution.py:8
  52.3 0.6 compare_reduce_fusion.3
  53.0 43.5 %all-gather.3.cloned.1.call-done = bf16[4,1024,512]{2,1,0:T(8,128)(2,1)} async-done(((bf16[4,32,512]{2,1,0:T(8,128)(2,1)}), bf16[4,1024,512]{2,1,0:T(8,128)(2,1)}) %all-gather.3.cloned.1.call-update) | async-done | bytes 4194320 | tf_op jit(solution)/shard_map/all_gather | solution.py:43
  96.5 4.7 copy.82
  101.2 5.0 %all-to-all-start = ((bf16[4,4,8,32,512]{4,3,1,0,2:T(8,128)(2,1)}), bf16[4,4,8,32,512]{4,3,1,0,2:T(8,128)(2,1)}, u32[]{:S(2)}, u32[]{:S(2)}) async-start(bf16[4,4,8,32,512]{4,3,1,0,2:T(8,128)(2,1)} %copy.82), calls=%async_computation | async-start | bytes 8388608 | tf_op jit(solution)/shard_map/all_to_all | solution.py:45
  106.2 0.6 compare_reduce_fusion.2
  108.2 4.0 while.4
  108.3 0.6 fusion.74
  108.8 1.4 bitcast_dynamic-update-slice_fusion.4
  110.3 0.6 fusion.74
  110.9 1.4 bitcast_dynamic-update-slice_fusion.4
  112.2 19.7 %custom-call.16 = f32[2,128,128]{1,2,0:T(8,128)S(1)} custom-call(f32[2,128,128]{2,1,0:T(8,128)S(1)} %get-tuple-element.21), custom_call_target="InvertDiagBlocksLowerTriangular" | custom-call | tf_op jit(solution)/shard_map/jit(_cho_solve)/triangular_solve | solution.py:10
  131.9 11.7 %cholesky.164 = f32[128,128]{1,0:T(8,128)S(1)} custom-call(f32[128,128]{1,0:T(8,128)S(1)} %cholesky.197), custom_call_target="Cholesky" | custom-call | tf_op jit(solution)/shard_map/jit(cholesky)/cholesky | solution.py:8
  143.7 9.8 %custom-call.17 = f32[1,128,128]{1,2,0:T(8,128)S(1)} custom-call(f32[1,128,128]{2,1,0:T(8,128)S(1)} %get-tuple-element.83), custom_call_target="InvertDiagBlocksLowerTriangular" | custom-call | tf_op jit(solution)/shard_map/jit(cholesky)/cholesky | solution.py:8
  153.7 0.3 convolution_subtract_fusion.4
  154.0 11.7 %cholesky.181 = f32[128,128]{1,0:T(8,128)S(1)} custom-call(f32[128,128]{1,0:T(8,128)S(1)} %convolution_subtract_fusion.4), custom_call_target="Cholesky" | custom-call | tf_op jit(solution)/shard_map/jit(cholesky)/cholesky | solution.py:8
  165.7 0.6 compare_reduce_fusion.1
  166.4 0.6 compare_reduce_fusion
  168.4 0.3 fusion.20
  168.7 0.3 convolution_subtract_fusion.3
  169.0 4.0 while.5
  169.0 0.6 fusion.75
  169.6 1.4 bitcast_dynamic-update-slice_fusion.5
  171.0 0.6 fusion.75
  171.6 1.4 bitcast_dynamic-update-slice_fusion.5
  173.0 2.5 copy.83
  175.5 9.8 %fusion.2 = f32[256,4,512]{2,0,1:T(8,128)} fusion(bf16[16,256,512,1]{2,1,0,3:T(8,128)(2,1)S(1)} %bitcast.134, bf16[4,256,16,256]{3,2,1,0:T(8,128)(2,1)} %bitcast.136), kind=kOutput, calls=%fused_computation.6 | convolution fusion | flops 4294967296 | bytes 14680064 | tf_op jit(solution)/shard_map/axcy,cyz->xaz/dot_general | solution.py:49
  185.4 0.3 fusion.35
  185.7 19.7 %custom-call.18 = f32[2,128,128]{1,2,0:T(8,128)S(1)} custom-call(f32[2,128,128]{2,1,0:T(8,128)S(1)} %get-tuple-element.22), custom_call_target="InvertDiagBlocksLowerTriangular" | custom-call | tf_op jit(solution)/shard_map/jit(_cho_solve)/triangular_solve | solution.py:10
  205.4 0.3 fusion.34
  205.7 0.3 fusion.18
  206.0 0.3 convolution_subtract_fusion.2
  206.3 0.3 convolution_subtract_fusion.1
  206.6 44.7 %all-reduce.7.cloned.1.call-done = f32[256,4,512]{2,0,1:T(8,128)} async-done(((f32[256,4,512]{2,0,1:T(8,128)}), f32[256,4,512]{2,0,1:T(8,128)}) %all-reduce.7.cloned.1.call-update) | async-done | bytes 2097168 | tf_op jit(solution)/shard_map/psum | solution.py:48
  251.3 1.0 fusion.15
  252.3 0.9 convolution_bitcast_fusion.3
  253.2 0.9 convolution_bitcast_fusion.2
  254.1 1.1 fusion.10
  255.2 0.9 convolution_bitcast_fusion.1
  256.2 0.3 fusion.33
  256.5 0.3 fusion.38
  256.8 0.3 fusion.37
  257.1 0.3 convolution_subtract_fusion
  257.4 149.9 %all-reduce.9.cloned.1.call-done = (f32[256,256]{1,0:T(8,128)}, f32[256,256]{1,0:T(8,128)}, f32[256,256]{1,0:T(8,128)}) async-done(((f32[256,256]{1,0:T(8,128)}, f32[256,256]{1,0:T(8,128)}, f32[256,256]{1,0:T(8,128)}), (f32[256,256]{1,0:T(8,128)}, f32[256,256]{1,0:T(8,128)}, f32[256,256]{1,0:T(8,128)})) %all-reduce.9.cloned.1.call-update) | async-done | bytes 786448 | tf_op jit(solution)/shard_map/psum | solution.py:72
  407.3 0.3 fusion.36
  407.6 1.6 fusion.71
  409.2 62.4 %all-reduce.11.cloned.1.call-done = (f32[256,256]{1,0:T(8,128)}, f32[256,256]{1,0:T(8,128)}, f32[256,256]{1,0:T(8,128)}) async-done(((f32[256,256]{1,0:T(8,128)}, f32[256,256]{1,0:T(8,128)}, f32[256,256]{1,0:T(8,128)}), (f32[256,256]{1,0:T(8,128)}, f32[256,256]{1,0:T(8,128)}, f32[256,256]{1,0:T(8,128)})) %all-reduce.11.cloned.1.call-update) | async-done | bytes 786448 | tf_op jit(solution)/shard_map/psum | solution.py:71
  471.6 1.0 maximum_subtract_fusion
  472.6 1.2 fusion.7
  473.9 1.9 fusion.6
  (48 shorter events, 2.2 us)
Async XLA Ops:
  7.2 247.0 %copy-start = (bf16[256,256]{1,0:T(8,128)(2,1)S(1)}, bf16[256,256]{1,0:T(8,128)(2,1)}, u32[]{:S(2)}) copy-start(bf16[256,256]{1,0:T(8,128)(2,1)} %param.16) | copy-start | bytes 393220
  7.2 89.3 %all-gather.3.cloned.1.call-start = ((), (), s32[]{:S(2)}) async-start(), calls=%async_computation.2 | async-start | bytes 4325376 | tf_op jit(solution)/shard_map/all_gather | solution.py:43
  101.2 71.8 %all-to-all-start = ((bf16[4,4,8,32,512]{4,3,1,0,2:T(8,128)(2,1)}), bf16[4,4,8,32,512]{4,3,1,0,2:T(8,128)(2,1)}, u32[]{:S(2)}, u32[]{:S(2)}) async-start(bf16[4,4,8,32,512]{4,3,1,0,2:T(8,128)(2,1)} %copy.82), calls=%async_computation | async-start | bytes 8388608 | tf_op jit(solution)/shard_map/all_to_all | solution.py:45
  106.2 145.1 %all-reduce.7.cloned.1.call-start = ((), (), s32[]{:S(2)}) async-start(), calls=%async_computation.1 | async-start | bytes 4194304 | tf_op jit(solution)/shard_map/psum | solution.py:48
  185.4 221.9 %all-reduce.9.cloned.1.call-start = ((), (), s32[]{:S(2)}) async-start(), calls=%async_computation.3 | async-start | bytes 1572864 | tf_op jit(solution)/shard_map/psum | solution.py:72
  255.2 220.6 %copy-start.3 = (bf16[32,4,256]{2,0,1:T(8,128)(2,1)}, bf16[32,4,256]{2,0,1:T(8,128)(2,1)S(1)}, u32[]{:S(2)}) copy-start(bf16[32,4,256]{2,0,1:T(8,128)(2,1)S(1)} %fusion.10) | copy-start | bytes 196612
  256.2 215.4 %all-reduce.11.cloned.1.call-start = ((), (), s32[]{:S(2)}) async-start(), calls=%async_computation.4 | async-start | bytes 1572864 | tf_op jit(solution)/shard_map/psum | solution.py:71
  472.6 3.2 copy-start.1
  473.9 2.0 copy-start.2
Sparse Core Ops, SparseCore 0:
  11.6 84.8 all-gather.2
  185.5 65.7 all-reduce.6
  256.3 150.9 all-reduce.8
  409.7 61.8 all-reduce.10
